TPU v7x, 256 devices: a whole 4x4x8 slice. The times are simulated.
256 devices in a mesh: tower: 4 (over x_lo, core), seq: 64 (over x_hi, z, y).
Axes of the slice: x: 4 (x_hi: 2, x_lo: 2; x = x_hi * 2 + x_lo), y: 4, z: 8, core: 2. Of those that a mesh axis runs over, the one named last changes fastest.
Arguments:
- queries: bfloat16 [4, 8192, 3072], P('tower', 'seq'), may hold values from -100 to 100
- keys: bfloat16 [4, 8192, 3072], P('tower', 'seq'), may hold values from -4 to 4
- values: bfloat16 [4, 8192, 3072], P('tower', 'seq'), may hold values from -6 to 6
- alignment: int32 [64, 2], replicated, may hold values from 0 to 192, as said below
- cross_gate: float32 [2, 24], replicated, may hold values from 0.5 to 2
Outputs:
- cross_out: bfloat16 [4, 8192, 3072], P('tower', 'seq')
Inputs may be any that keep to these rules, and one draw needn't show every extreme that they name: `alignment`: lo[a] is max(3a - 1, 0) or max(3a, 0); hi[a] is min(3a + 3, 192) or min(3a + 4, 192).
All inputs are finite; a program needn't handle non-finite values.
Results may differ from a plain program's by a relative error of at most 0.0044.
Values may be sent and summed in bfloat16 or wider, within the bound.
A program may use at most 128 MiB of HBM per device.

v0:
```python
import jax
import jax.numpy as jnp
from jax import lax
from jax.sharding import PartitionSpec as P

HEADS = 24
HEAD_DIM = 128
BLOCK = 128


def from_behind(block, axis, distance):
    devices = range(lax.axis_size(axis))
    route = [(i - distance, i) for i in devices if i - distance in devices]
    return lax.ppermute(block, axis, route)


def attend(query_block, key_rows, value_rows, valid, gain):
    count_q = query_block.shape[0]
    count_k = key_rows.shape[0]
    q_heads = query_block.reshape(count_q, HEADS, HEAD_DIM)
    k_heads = key_rows.reshape(count_k, HEADS, HEAD_DIM)
    v_heads = value_rows.reshape(count_k, HEADS, HEAD_DIM)
    scores = jnp.einsum(
        "qhd,khd->hqk", q_heads, k_heads, preferred_element_type=jnp.float32
    ) * HEAD_DIM ** (-0.5)
    scores = jnp.where(valid[None, None, :], scores, -jnp.inf)
    top = jnp.max(scores, axis=2, keepdims=True)
    weights = jnp.exp(scores - top)
    total = jnp.sum(weights, axis=2)
    rounded = weights.astype(jnp.bfloat16)
    mixed = jnp.einsum("hqk,khd->qhd", rounded, v_heads, preferred_element_type=jnp.float32)
    mixed = mixed / jnp.transpose(total)[:, :, None] * gain[None, :, None]
    return mixed.reshape(count_q, HEADS * HEAD_DIM)


def local(queries, keys, values, alignment, cross_gate):
    rows = queries.shape[1]
    per_dev = rows // BLOCK
    seq_count = lax.axis_size("seq")
    column = lax.axis_index("seq")
    section = lax.axis_index("tower")
    lows = alignment[:, 0]
    highs = alignment[:, 1]
    video_total = 3 * per_dev * seq_count
    audio_total = per_dev * seq_count
    local_queries = queries[0]

    def video_path(audio_keys, audio_values):

        def video_step(block):
            index = per_dev * (3 * column + section) + block
            first = index // 3 - 1
            near = first + jnp.arange(3, dtype=jnp.int32)
            safe = jnp.clip(near, 0, audio_total - 1)
            linked = (
                (near >= 0)
                & (near < audio_total)
                & (jnp.take(lows, safe) <= index)
                & (index < jnp.take(highs, safe))
            )
            return attend(
                local_queries, audio_keys, audio_values, jnp.repeat(linked, BLOCK), cross_gate[0]
            )

        return lax.map(video_step, jnp.arange(per_dev, dtype=jnp.int32))

    key_all, value_all = (
        lax.all_gather(keys, "tower", axis=0, tiled=True),
        lax.all_gather(values, "tower", axis=0, tiled=True),
    )
    lower_pack = jnp.stack(
        [
            jnp.stack([key_all[2, rows - BLOCK :], key_all[3, rows - BLOCK :]]),
            jnp.stack([value_all[2, rows - BLOCK :], value_all[3, rows - BLOCK :]]),
        ]
    )
    upper_pack = jnp.stack(
        [
            jnp.stack([key_all[0, :BLOCK], key_all[3, :BLOCK]]),
            jnp.stack([value_all[0, :BLOCK], value_all[3, :BLOCK]]),
        ]
    )
    lower = from_behind(lower_pack, "seq", 1)
    upper = from_behind(upper_pack, "seq", -1)
    lower_video, lower_audio = (lower[:, 0], lower[:, 1])
    upper_video, upper_audio = (upper[:, 0], upper[:, 1])
    video_keys = jnp.concatenate(
        [lower_video[0], key_all[0], key_all[1], key_all[2], upper_video[0]], axis=0
    )
    video_values = jnp.concatenate(
        [lower_video[1], value_all[0], value_all[1], value_all[2], upper_video[1]], axis=0
    )
    audio_keys = jnp.concatenate([lower_audio[0], key_all[3], upper_audio[0]], axis=0)
    audio_values = jnp.concatenate([lower_audio[1], value_all[3], upper_audio[1]], axis=0)

    def audio_path(unused):

        def audio_step(block):
            index = per_dev * column + block
            first = 3 * index - 1
            near = first + jnp.arange(5, dtype=jnp.int32)
            linked = (
                (near >= 0)
                & (near < video_total)
                & (jnp.take(lows, index) <= near)
                & (near < jnp.take(highs, index))
            )
            return attend(
                local_queries, video_keys, video_values, jnp.repeat(linked, BLOCK), cross_gate[1]
            )

        return lax.map(audio_step, jnp.arange(per_dev, dtype=jnp.int32))

    mixed = lax.cond(
        section == 3, audio_path, lambda unused: video_path(audio_keys, audio_values), 0
    )
    return mixed.astype(jnp.bfloat16)


def solution(mesh):
    placed = (P("tower", "seq", None), P("tower", "seq", None), P("tower", "seq", None), P(), P())
    return jax.shard_map(
        local, mesh=mesh, in_specs=placed, out_specs=P("tower", "seq", None), check_vma=False
    )
```

profile of v0, /device:TPU:7, one launch (start us, length us, event | category | flops | bytes accessed | tf_op | source)
XLA Modules:
  0.0 233.7 jit_solution(7783236076697758818)
XLA Ops:
  6.5 0.0 all-gather.5.cloned.1.call-start
  6.5 0.7 all-gather.5.cloned.1.call-update
  7.3 0.0 all-gather.3.cloned.1.call-start
  7.3 0.7 all-gather.3.cloned.1.call-update
  8.0 44.2 %all-gather.5.cloned.1.call-done = bf16[4,128,3072]{2,1,0:T(8,128)(2,1)} async-done(((bf16[1,128,3072]{2,1,0:T(8,128)(2,1)}), bf16[4,128,3072]{2,1,0:T(8,128)(2,1)}) %all-gather.5.cloned.1.call-update) | async-done | bytes 3145744 | tf_op jit(solution)/shard_map/all_gather | solution.py:69
  52.2 2.5 %slice_bitcast_fusion.18 = (bf16[128,3072]{1,0:T(8,128)(2,1)}, bf16[1,128,3072]{2,1,0:T(8,128)(2,1)S(1)}, bf16[1,128,3072]{2,1,0:T(8,128)(2,1)S(1)}) fusion(bf16[4,128,3072]{2,1,0:T(8,128)(2,1)} %all-gather.5.cloned.1.call-done), kind=kLoop, calls=%fused_computation.80 | loop fusion | bytes 3932160 | tf_op jit(solution)/shard_map/squeeze | solution.py:94
  54.8 40.5 %all-gather.3.cloned.1.call-done = bf16[4,128,3072]{2,1,0:T(8,128)(2,1)} async-done(((bf16[1,128,3072]{2,1,0:T(8,128)(2,1)}), bf16[4,128,3072]{2,1,0:T(8,128)(2,1)}) %all-gather.3.cloned.1.call-update) | async-done | bytes 3145744 | tf_op jit(solution)/shard_map/all_gather | solution.py:68
  95.3 2.5 %slice_bitcast_fusion.19 = (bf16[128,3072]{1,0:T(8,128)(2,1)}, bf16[1,128,3072]{2,1,0:T(8,128)(2,1)S(1)}, bf16[1,128,3072]{2,1,0:T(8,128)(2,1)S(1)}) fusion(bf16[4,128,3072]{2,1,0:T(8,128)(2,1)} %all-gather.3.cloned.1.call-done), kind=kLoop, calls=%fused_computation.81 | loop fusion | bytes 3932160 | tf_op jit(solution)/shard_map/squeeze | solution.py:93
  97.8 0.3 maximum_bitcast_fusion
  98.0 0.0 copy-start.1
  98.0 0.0 copy-start.2
  98.1 1.9 pad_maximum_fusion.1
  100.0 8.0 %collective-permute-start.1 = (bf16[2,2,128,3072]{3,2,1,0:T(8,128)(2,1)}, bf16[2,2,128,3072]{3,2,1,0:T(8,128)(2,1)}, u32[]{:S(2)}, u32[]{:S(2)}) collective-permute-start(bf16[2,2,128,3072]{3,2,1,0:T(8,128)(2,1)} %pad_maximum_fusion.1), channel_id=1, source_target_pairs={{1,0},{2,1},{3,2},{4,3},{5,4},{6,5},{7,6},{8,7},{9,8},{10,9},{11,1... | collective-permute-start | bytes 9437192 | tf_op jit(solution)/shard_map/ppermute | solution.py:14
  107.9 0.0 copy-done.1
  107.9 0.1 slice_bitcast_fusion.2
  108.1 0.0 copy-done.2
  108.1 0.1 slice_bitcast_fusion.3
  108.2 0.0 copy-start.9
  108.2 2.0 pad_maximum_fusion
  110.1 1.9 collective-permute-start
  112.1 0.0 copy-done.9
  112.1 0.0 copy-start.7
  112.1 63.8 %collective-permute-done.1 = bf16[2,2,128,3072]{3,2,1,0:T(8,128)(2,1)} collective-permute-done((bf16[2,2,128,3072]{3,2,1,0:T(8,128)(2,1)}, bf16[2,2,128,3072]{3,2,1,0:T(8,128)(2,1)}, u32[]{:S(2)}, u32[]{:S(2)}) %collective-permute-start.1) | collective-permute-done | bytes 3145760 | tf_op jit(solution)/shard_map/ppermute | solution.py:14
  176.0 1.5 slice_bitcast_fusion.12
  177.4 0.0 copy-start.8
  177.4 10.3 %collective-permute-done = bf16[2,2,128,3072]{3,2,1,0:T(8,128)(2,1)} collective-permute-done((bf16[2,2,128,3072]{3,2,1,0:T(8,128)(2,1)}, bf16[2,2,128,3072]{3,2,1,0:T(8,128)(2,1)}, u32[]{:S(2)}, u32[]{:S(2)}) %collective-permute-start) | collective-permute-done | bytes 3145760 | tf_op jit(solution)/shard_map/ppermute | solution.py:14
  187.7 1.5 slice_bitcast_fusion.13
  189.2 0.0 copy-done.7
  189.2 1.6 pad_maximum_fusion.3
  190.8 0.0 copy-done.8
  190.8 0.0 copy-start.3
  190.8 1.6 pad_maximum_fusion.2
  192.4 2.8 %fusion.39 = (bf16[640,3072]{1,0:T(8,128)(2,1)}, bf16[640,3072]{1,0:T(8,128)(2,1)}) fusion(bf16[2,2,128,3072]{3,2,1,0:T(8,128)(2,1)} %collective-permute-done), kind=kLoop, calls=%fused_computation.63 | loop fusion | bytes 3145728
  195.2 0.0 copy-done.3
  195.2 1.2 bitcast_dynamic-update-slice_fusion
  196.4 0.9 fusion.38
  197.4 0.0 copy-start.10
  197.4 1.0 fusion.37
  198.3 0.0 copy-start.4
  198.3 0.0 copy-start.6
  198.3 0.9 fusion.42
  199.3 1.0 fusion.41
  200.2 2.6 %fusion.36 = (bf16[640,3072]{1,0:T(8,128)(2,1)}, bf16[640,3072]{1,0:T(8,128)(2,1)}) fusion(bf16[640,3072]{1,0:T(8,128)(2,1)} %fusion.37, bf16[2,2,128,3072]{3,2,1,0:T(8,128)(2,1)} %collective-permute-done.1, bf16[640,3072]{1,0:T(8,128)(2,1)} %fusion.41), kind=kLoop, calls=%fused_computation.57 | loop fusion | bytes 3145728 | tf_op jit(solution)/shard_map/concatenate | solution.py:90
  202.8 0.0 copy-done.10
  202.8 0.0 copy-done.4
  202.8 0.0 copy-done.6
  202.8 22.9 %conditional.6 = (bf16[1,128,3072]{1,2,0:T(8,128)(2,1)S(1)}) conditional(s32[]{:T(128)} %convert_element_type.28, (s32[]{:T(128)}, s32[]{:T(128)}, s32[64]{0:T(128)S(1)}, s32[64]{0:T(128)S(1)}, bf16[1,128,3072]{2,1,0:T(8,128)(2,1)S(1)}, /*index=5*/bf16[384,3072]{1,0:T(8,128)(2,1)}, bf16[384,3072]{1,0:T(8,128)(2,1)S(1)}, ...), branch_computations={%region_0.4_spmd, %region_3.7_spmd} | conditional | flops 1029433408 | bytes 73989080
  203.0 0.6 dynamic-slice.4
  204.3 0.6 dynamic-slice.5
  205.4 0.1 broadcast_bitcast_fusion
  205.5 0.2 copy.32
  205.7 3.8 %fusion = (f32[24,128]{1,0:T(8,128)S(1)}, f32[24,128,640]{2,1,0:T(8,128)S(1)}) fusion(pred[640]{0:T(1024)(128)(4,1)S(1)} %broadcast_bitcast_fusion, bf16[128,24,128]{2,1,0:T(8,128)(2,1)S(1)} %bitcast.114, bf16[640,3072]{1,0:T(8,128)(2,1)} %get-tuple-element.114), kind=kOutput, calls=%fused_computation.4 | convolution fusion | flops 509211648 | bytes 12595840 | tf_op jit(solution)/shard_map/cond/branch_1_fun/while/body/eval_jaxpr/qhd,khd->hqk/dot_general | solution.py:23
  209.5 0.0 copy-start
  209.5 2.0 fusion.1
  211.5 1.2 copy-done
  212.7 6.2 %copy.29 = bf16[640,3072]{0,1:T(8,128)(2,1)} copy(bf16[640,3072]{1,0:T(8,128)(2,1)} %get-tuple-element.182) | data formatting | bytes 7864320 | tf_op jit(solution)/shard_map
  218.8 6.9 %fusion.12 = bf16[128,24,128]{0,2,1:T(8,128)(2,1)S(1)} fusion(bf16[640,24,128]{0,2,1:T(8,128)(2,1)} %bitcast.111, f32[24,128,640]{2,1,0:T(8,128)} %copy-done, f32[24,128]{1,0:T(8,128)S(1)} %get-tuple-element.184, pred[640]{0:T(1024)(128)(4,1)S(1)} %broadcast_bitcast_fusion, f32[24]{0:T(128)S(1)} %slice_bitcast_fusion, f32[128,24]{0,1:T(8,128)S(1)} %bitcast.120), kind=kOutput, calls=%fused_computation.16 | convolution fusion | flops 512360448 | bytes 12608224 | tf_op jit(solution)/shard_map/cond/branch_1_fun/while/body/eval_jaxpr/hqk,khd->qhd/dot_general | solution.py:31
  225.7 1.2 copy.30
  (3 shorter events, 0.0 us)
Async XLA Ops:
  6.5 45.7 %all-gather.5.cloned.1.call-start = ((), (), s32[]{:S(2)}) async-start(), calls=%async_computation.1 | async-start | bytes 3932160 | tf_op jit(solution)/shard_map/all_gather | solution.py:69
  7.3 88.0 %all-gather.3.cloned.1.call-start = ((), (), s32[]{:S(2)}) async-start(), calls=%async_computation | async-start | bytes 3932160 | tf_op jit(solution)/shard_map/all_gather | solution.py:68
  98.0 9.9 %copy-start.1 = (bf16[4,128,3072]{2,1,0:T(8,128)(2,1)S(1)}, bf16[4,128,3072]{2,1,0:T(8,128)(2,1)}, u32[]{:S(2)}) copy-start(bf16[4,128,3072]{2,1,0:T(8,128)(2,1)} %all-gather.5.cloned.1.call-done) | copy-start | bytes 9437188
  98.0 10.0 %copy-start.2 = (bf16[4,128,3072]{2,1,0:T(8,128)(2,1)S(1)}, bf16[4,128,3072]{2,1,0:T(8,128)(2,1)}, u32[]{:S(2)}) copy-start(bf16[4,128,3072]{2,1,0:T(8,128)(2,1)} %all-gather.3.cloned.1.call-done) | copy-start | bytes 9437188
  100.0 76.0 %collective-permute-start.1 = (bf16[2,2,128,3072]{3,2,1,0:T(8,128)(2,1)}, bf16[2,2,128,3072]{3,2,1,0:T(8,128)(2,1)}, u32[]{:S(2)}, u32[]{:S(2)}) collective-permute-start(bf16[2,2,128,3072]{3,2,1,0:T(8,128)(2,1)} %pad_maximum_fusion.1), channel_id=1, source_target_pairs={{1,0},{2,1},{3,2},{4,3},{5,4},{6,5},{7,6},{8,7},{9,8},{10,9},{11,1... | collective-permute-start | bytes 9437192 | tf_op jit(solution)/shard_map/ppermute | solution.py:14
  108.2 3.9 %copy-start.9 = (s32[64,2]{0,1:T(2,128)S(1)}, s32[64,2]{0,1:T(2,128)}, u32[]{:S(2)}) copy-start(s32[64,2]{0,1:T(2,128)} %param.12) | copy-start | bytes 1540
  110.1 77.6 %collective-permute-start = (bf16[2,2,128,3072]{3,2,1,0:T(8,128)(2,1)}, bf16[2,2,128,3072]{3,2,1,0:T(8,128)(2,1)}, u32[]{:S(2)}, u32[]{:S(2)}) collective-permute-start(bf16[2,2,128,3072]{3,2,1,0:T(8,128)(2,1)} %pad_maximum_fusion), channel_id=1, source_target_pairs={{0,1},{1,2},{2,3},{3,4},{4,5},{5,6},{6,7},{7,8},{8,9},{9,10},{10,1... | collective-permute-start | bytes 9437192 | tf_op jit(solution)/shard_map/ppermute | solution.py:14
  112.1 77.1 %copy-start.7 = (bf16[128,3072]{1,0:T(8,128)(2,1)S(1)}, bf16[128,3072]{1,0:T(8,128)(2,1)}, u32[]{:S(2)}) copy-start(bf16[128,3072]{1,0:T(8,128)(2,1)} %get-tuple-element.194) | copy-start | bytes 2359300
  177.4 13.3 %copy-start.8 = (bf16[128,3072]{1,0:T(8,128)(2,1)S(1)}, bf16[128,3072]{1,0:T(8,128)(2,1)}, u32[]{:S(2)}) copy-start(bf16[128,3072]{1,0:T(8,128)(2,1)} %get-tuple-element.199) | copy-start | bytes 2359300
  190.8 4.4 %copy-start.3 = (bf16[4,128,3072]{2,1,0:T(8,128)(2,1)S(1)}, bf16[4,128,3072]{2,1,0:T(8,128)(2,1)}, u32[]{:S(2)}) copy-start(bf16[4,128,3072]{2,1,0:T(8,128)(2,1)} %all-gather.3.cloned.1.call-done) | copy-start | bytes 9437188
  197.4 5.5 %copy-start.10 = (f32[2,24]{1,0:T(2,128)S(1)}, f32[2,24]{1,0:T(2,128)}, u32[]{:S(2)}) copy-start(f32[2,24]{1,0:T(2,128)} %param.13) | copy-start | bytes 580
  198.3 4.5 %copy-start.4 = (bf16[384,3072]{1,0:T(8,128)(2,1)S(1)}, bf16[384,3072]{1,0:T(8,128)(2,1)}, u32[]{:S(2)}) copy-start(bf16[384,3072]{1,0:T(8,128)(2,1)} %pad_maximum_fusion.3) | copy-start | bytes 7077892
  198.3 4.5 %copy-start.6 = (bf16[1,128,3072]{2,1,0:T(8,128)(2,1)S(1)}, bf16[1,128,3072]{2,1,0:T(8,128)(2,1)}, u32[]{:S(2)}) copy-start(bf16[1,128,3072]{2,1,0:T(8,128)(2,1)} %param.9) | copy-start | bytes 2359300
  209.5 3.1 %copy-start = (f32[24,128,640]{2,1,0:T(8,128)}, f32[24,128,640]{2,1,0:T(8,128)S(1)}, u32[]{:S(2)}) copy-start(f32[24,128,640]{2,1,0:T(8,128)S(1)} %get-tuple-element.185) | copy-start | bytes 23592964 | tf_op jit(solution)/shard_map/conditional.1
Sparse Core Ops, SparseCore 0:
  9.1 43.0 all-gather.4
  54.0 41.2 all-gather.2
where the time goes:
time: 234 us
  waiting for transfers between devices  160 us (68%)
  local copies, waits for them, and re-layouts  28.5 us (12%)
  between operations  13.5 us (6%)
  matrix products  10.7 us (5%)
  starting transfers between devices  9.92 us (4%)
  other arithmetic  9.3 us (4%)
    ppermute x2, waiting for transfers between devices, from_behind(): return lax.ppermute(block, axis, route)  74.1 us
    all_gather x1, waiting for transfers between devices, local(): lax.all_gather(values, 'tower', axis=0, tiled=True)  44.2 us
    all_gather x1, waiting for transfers between devices, local(): lax.all_gather(keys, 'tower', axis=0, tiled=True)  40.5 us
    ppermute x2, starting transfers between devices, from_behind(): return lax.ppermute(block, axis, route)  9.87 us
    unnamed x24, local copies, waits for them, and re-layouts  7.85 us
    another operation x4, local copies, waits for them, and re-layouts  7.48 us
    dot_general x1, matrix products, attend(): jnp.einsum('hqk,khd->qhd', rounded, v_heads, preferred_element_type=jnp.f...  6.88 us
  transfers between devices with their start and end apart: 4, of which 4 were waited for; matrix products, arithmetic and copies ran while one was open for 3% of the time, Pallas kernels for 0%

commit v1 on v0

--- a/solution.py
+++ b/solution.py
@@ -6,6 +6,13 @@
 HEADS = 24
 HEAD_DIM = 128
 BLOCK = 128
+
+
+def gather_over(x, axis, along):
+    n_dev = lax.axis_size(axis)
+    tiles = jnp.stack([x for _ in range(n_dev)])
+    tiles = lax.all_to_all(tiles, axis, split_axis=0, concat_axis=0)
+    return jnp.concatenate(tiles, axis=along)
 
 
 def from_behind(block, axis, distance):
@@ -66,7 +73,7 @@
 
     key_all, value_all = (
         lax.all_gather(keys, "tower", axis=0, tiled=True),
-        lax.all_gather(values, "tower", axis=0, tiled=True),
+        gather_over(values, "tower", 0),
     )
     lower_pack = jnp.stack(
         [

time: 234 us -> 215 us (0.919)
  waiting for transfers between devices: 160 us -> 75.8 us
  blocking collectives: 0 us -> 59.1 us
  starting transfers between devices: 9.92 us -> 13.4 us
    all_to_all x0 -> x1, blocking collectives: none -> 59.1 us  [gather_over(): tiles = lax.all_to_all(tiles, axis, split_axis=0, concat_axis=0)]
    all_gather x1 -> x0, waiting for transfers between devices: 44.2 us -> none  [local(): lax.all_gather(values, 'tower', axis=0, tiled=True)]
    all_gather x1, waiting for transfers between devices: 40.5 us -> 2.05 us  [local(): lax.all_gather(keys, 'tower', axis=0, tiled=True)]
    ppermute x2, starting transfers between devices: 9.87 us -> 13.4 us  [from_behind(): return lax.ppermute(block, axis, route)]
    another operation x4 -> x5, local copies, waits for them, and re-layouts: 7.48 us -> 10.2 us
    unnamed x24 -> x22, local copies, waits for them, and re-layouts: 7.85 us -> 7.76 us
  transfers between devices with their start and end apart: 4 -> 3, of which waited for: 4 -> 3; matrix products, arithmetic and copies ran while one was open for 3% -> 4% of each run, Pallas kernels for 0% -> 0%
where the time goes in v1:
time: 215 us
  waiting for transfers between devices  75.8 us (35%)
  blocking collectives  59.1 us (27%)
  local copies, waits for them, and re-layouts  30.1 us (14%)
  between operations  13.6 us (6%)
  starting transfers between devices  13.4 us (6%)
  matrix products  10.7 us (5%)
  other arithmetic  10.6 us (5%)
    ppermute x2, waiting for transfers between devices, from_behind(): return lax.ppermute(block, axis, route)  73 us
    all_to_all x1, blocking collectives, gather_over(): tiles = lax.all_to_all(tiles, axis, split_axis=0, concat_axis=0)  59.1 us
    ppermute x2, starting transfers between devices, from_behind(): return lax.ppermute(block, axis, route)  13.4 us
    another operation x4, local copies, waits for them, and re-layouts  8.71 us
    unnamed x22, local copies, waits for them, and re-layouts  7.76 us
    dot_general x1, matrix products, attend(): jnp.einsum('hqk,khd->qhd', rounded, v_heads, preferred_element_type=jnp.f...  6.88 us
  transfers between devices with their start and end apart: 3, of which 3 were waited for; matrix products, arithmetic and copies ran while one was open for 4% of the time, Pallas kernels for 0%

profile of v1, /device:TPU:7, one launch (start us, length us, event | category | flops | bytes accessed | tf_op | source)
XLA Modules:
  0.0 214.5 jit_solution(9601372963733712683)
XLA Ops:
  6.5 0.0 all-gather.2.cloned.1.call-start
  6.5 0.7 all-gather.2.cloned.1.call-update
  7.3 1.5 stack.39
  8.8 59.1 %all_to_all.5 = bf16[4,1,128,3072]{3,2,1,0:T(8,128)(2,1)S(1)} all-to-all(bf16[4,1,128,3072]{3,2,1,0:T(8,128)(2,1)S(1)} %stack.39), channel_id=1, replica_groups=mesh['tower'=4,'seq'=64] {'tower'}, dimensions={0} | all-to-all | bytes 6291456 | tf_op jit(solution)/shard_map/all_to_all | solution.py:14
  67.8 1.2 slice_bitcast_fusion.15
  69.0 1.9 fusion.36
  70.9 2.1 all-gather.2.cloned.1.call-done
  73.0 0.0 copy-start.5
  73.0 2.7 %slice_bitcast_fusion.20 = (bf16[128,3072]{1,0:T(8,128)(2,1)}, bf16[1,128,3072]{2,1,0:T(8,128)(2,1)S(1)}, bf16[1,128,3072]{2,1,0:T(8,128)(2,1)S(1)}) fusion(bf16[4,128,3072]{2,1,0:T(8,128)(2,1)} %all-gather.2.cloned.1.call-done), kind=kLoop, calls=%fused_computation.85 | loop fusion | bytes 3932160 | tf_op jit(solution)/shard_map/squeeze | solution.py:100
  75.7 0.1 maximum_bitcast_fusion
  75.9 0.0 copy-start.1
  75.9 0.0 copy-done.5
  75.9 0.0 copy-start.4
  75.9 2.0 pad_maximum_fusion.1
  77.9 11.5 %collective-permute-start.1 = (bf16[2,2,128,3072]{3,2,1,0:T(8,128)(2,1)}, bf16[2,2,128,3072]{3,2,1,0:T(8,128)(2,1)}, u32[]{:S(2)}, u32[]{:S(2)}) collective-permute-start(bf16[2,2,128,3072]{3,2,1,0:T(8,128)(2,1)} %pad_maximum_fusion.1), channel_id=1, source_target_pairs={{1,0},{2,1},{3,2},{4,3},{5,4},{6,5},{7,6},{8,7},{9,8},{10,9},{11,1... | collective-permute-start | bytes 9437192 | tf_op jit(solution)/shard_map/ppermute | solution.py:21
  89.4 0.0 copy-done.1
  89.4 0.1 slice_bitcast_fusion.2
  89.5 0.0 copy-start.9
  89.5 0.0 copy-done.4
  89.5 1.9 pad_maximum_fusion
  91.4 1.9 collective-permute-start
  93.4 0.0 copy-done.9
  93.4 0.0 copy-start.7
  93.4 0.0 copy-start.8
  93.4 62.9 %collective-permute-done.1 = bf16[2,2,128,3072]{3,2,1,0:T(8,128)(2,1)} collective-permute-done((bf16[2,2,128,3072]{3,2,1,0:T(8,128)(2,1)}, bf16[2,2,128,3072]{3,2,1,0:T(8,128)(2,1)}, u32[]{:S(2)}, u32[]{:S(2)}) %collective-permute-start.1) | collective-permute-done | bytes 3145760 | tf_op jit(solution)/shard_map/ppermute | solution.py:21
  156.3 1.5 slice_bitcast_fusion.10
  157.7 10.2 %collective-permute-done = bf16[2,2,128,3072]{3,2,1,0:T(8,128)(2,1)} collective-permute-done((bf16[2,2,128,3072]{3,2,1,0:T(8,128)(2,1)}, bf16[2,2,128,3072]{3,2,1,0:T(8,128)(2,1)}, u32[]{:S(2)}, u32[]{:S(2)}) %collective-permute-start) | collective-permute-done | bytes 3145760 | tf_op jit(solution)/shard_map/ppermute | solution.py:21
  167.9 1.5 slice_bitcast_fusion.11
  169.4 0.0 copy-done.7
  169.4 0.0 copy-done.8
  169.4 0.0 copy-start.2
  169.4 2.6 %pad_maximum_fusion.2 = (bf16[384,3072]{1,0:T(8,128)(2,1)}, bf16[384,3072]{1,0:T(8,128)(2,1)}) fusion(bf16[128,3072]{1,0:T(8,128)(2,1)S(1)} %get-tuple-element.199, bf16[128,3072]{1,0:T(8,128)(2,1)S(1)} %copy-done.8, bf16[128,3072]{1,0:T(8,128)(2,1)S(1)} %get-tuple-element.193, bf16[128,3072]{1,0:T(8,128)(2,1)S(1)} %get-tuple-element.198, ...), kind=kLoop, calls=%fused_computation.50 | loop fusion | flops 14155776 | bytes 9437184 | tf_op jit(solution)/shard_map/concatenate | solution.py:100
  172.0 2.7 %fusion.40 = (bf16[640,3072]{1,0:T(8,128)(2,1)}, bf16[640,3072]{1,0:T(8,128)(2,1)}) fusion(bf16[2,2,128,3072]{3,2,1,0:T(8,128)(2,1)} %collective-permute-done), kind=kLoop, calls=%fused_computation.63 | loop fusion | bytes 3145728
  174.7 0.0 copy-done.2
  174.7 1.3 bitcast_dynamic-update-slice_fusion.1
  176.0 1.0 fusion.43
  176.9 0.0 copy-start.10
  176.9 1.0 fusion.42
  177.9 0.9 fusion.39
  178.8 0.9 bitcast_dynamic-update-slice_fusion
  179.7 2.6 %fusion.38 = (bf16[640,3072]{1,0:T(8,128)(2,1)}, bf16[640,3072]{1,0:T(8,128)(2,1)}) fusion(bf16[640,3072]{1,0:T(8,128)(2,1)} %bitcast_dynamic-update-slice_fusion, bf16[2,2,128,3072]{3,2,1,0:T(8,128)(2,1)} %collective-permute-done.1, bf16[640,3072]{1,0:T(8,128)(2,1)} %fusion.42), kind=kLoop, calls=%fused_computation.59 | loop fusion | bytes 3145728 | tf_op jit(solution)/shard_map/concatenate | solution.py:97
  182.4 0.0 copy-done.10
  182.4 24.1 %conditional.6 = (bf16[1,128,3072]{1,2,0:T(8,128)(2,1)S(1)}) conditional(s32[]{:T(128)} %convert_element_type.28, (s32[]{:T(128)}, s32[]{:T(128)}, s32[64]{0:T(128)S(1)}, s32[64]{0:T(128)S(1)}, bf16[1,128,3072]{2,1,0:T(8,128)(2,1)}, /*index=5*/bf16[384,3072]{1,0:T(8,128)(2,1)}, bf16[384,3072]{1,0:T(8,128)(2,1)}, f32[2,24]{1,0:T(2,128)S(1)}) %tuple.63, ...), branch_computations={%region_0.4_spmd, %region_3.7_spmd} | conditional | flops 1029433408 | bytes 73989080
  182.4 0.6 dynamic-slice.4
  183.6 0.7 dynamic-slice.5
  185.0 0.1 broadcast_bitcast_fusion
  185.1 1.3 copy.32
  186.3 3.8 %fusion = (f32[24,128]{1,0:T(8,128)S(1)}, f32[24,128,640]{2,1,0:T(8,128)S(1)}) fusion(pred[640]{0:T(1024)(128)(4,1)S(1)} %broadcast_bitcast_fusion, bf16[128,24,128]{2,1,0:T(8,128)(2,1)S(1)} %bitcast.119, bf16[640,3072]{1,0:T(8,128)(2,1)} %get-tuple-element.114), kind=kOutput, calls=%fused_computation.4 | convolution fusion | flops 509211648 | bytes 12595840 | tf_op jit(solution)/shard_map/cond/branch_1_fun/while/body/eval_jaxpr/qhd,khd->hqk/dot_general | solution.py:30
  190.2 0.0 copy-start
  190.2 2.0 fusion.1
  192.2 1.1 copy-done
  193.2 6.4 %copy.29 = bf16[640,3072]{0,1:T(8,128)(2,1)} copy(bf16[640,3072]{1,0:T(8,128)(2,1)} %get-tuple-element.182) | data formatting | bytes 7864320 | tf_op jit(solution)/shard_map
  199.6 6.9 %fusion.12 = bf16[128,24,128]{0,2,1:T(8,128)(2,1)S(1)} fusion(bf16[640,24,128]{0,2,1:T(8,128)(2,1)} %bitcast.116, f32[24,128,640]{2,1,0:T(8,128)} %copy-done, f32[24,128]{1,0:T(8,128)S(1)} %get-tuple-element.184, pred[640]{0:T(1024)(128)(4,1)S(1)} %broadcast_bitcast_fusion, f32[24]{0:T(128)S(1)} %slice_bitcast_fusion, f32[128,24]{0,1:T(8,128)S(1)} %bitcast.126), kind=kOutput, calls=%fused_computation.16 | convolution fusion | flops 512360448 | bytes 12608224 | tf_op jit(solution)/shard_map/cond/branch_1_fun/while/body/eval_jaxpr/hqk,khd->qhd/dot_general | solution.py:38
  206.5 1.2 copy.30
  (3 shorter events, 0.0 us)
Async XLA Ops:
  6.5 66.5 %all-gather.2.cloned.1.call-start = ((), (), s32[]{:S(2)}) async-start(), calls=%async_computation.1 | async-start | bytes 3932160 | tf_op jit(solution)/shard_map/all_gather | solution.py:75
  73.0 2.9 %copy-start.5 = (bf16[1,2,128,3072]{3,2,1,0:T(8,128)(2,1)S(1)}, bf16[1,2,128,3072]{3,2,1,0:T(8,128)(2,1)}, u32[]{:S(2)}) copy-start(bf16[1,2,128,3072]{3,2,1,0:T(8,128)(2,1)} %get-tuple-element.204) | copy-start | bytes 4718596
  75.9 13.5 %copy-start.1 = (bf16[4,128,3072]{2,1,0:T(8,128)(2,1)S(1)}, bf16[4,128,3072]{2,1,0:T(8,128)(2,1)}, u32[]{:S(2)}) copy-start(bf16[4,128,3072]{2,1,0:T(8,128)(2,1)} %all-gather.2.cloned.1.call-done) | copy-start | bytes 9437188
  75.9 13.6 %copy-start.4 = (bf16[1,2,128,3072]{3,2,1,0:T(8,128)(2,1)S(1)}, bf16[1,2,128,3072]{3,2,1,0:T(8,128)(2,1)}, u32[]{:S(2)}) copy-start(bf16[1,2,128,3072]{3,2,1,0:T(8,128)(2,1)} %get-tuple-element.203) | copy-start | bytes 4718596
  77.9 78.4 %collective-permute-start.1 = (bf16[2,2,128,3072]{3,2,1,0:T(8,128)(2,1)}, bf16[2,2,128,3072]{3,2,1,0:T(8,128)(2,1)}, u32[]{:S(2)}, u32[]{:S(2)}) collective-permute-start(bf16[2,2,128,3072]{3,2,1,0:T(8,128)(2,1)} %pad_maximum_fusion.1), channel_id=1, source_target_pairs={{1,0},{2,1},{3,2},{4,3},{5,4},{6,5},{7,6},{8,7},{9,8},{10,9},{11,1... | collective-permute-start | bytes 9437192 | tf_op jit(solution)/shard_map/ppermute | solution.py:21
  89.5 3.9 %copy-start.9 = (s32[64,2]{0,1:T(2,128)S(1)}, s32[64,2]{0,1:T(2,128)}, u32[]{:S(2)}) copy-start(s32[64,2]{0,1:T(2,128)} %param.12) | copy-start | bytes 1540
  91.4 76.5 %collective-permute-start = (bf16[2,2,128,3072]{3,2,1,0:T(8,128)(2,1)}, bf16[2,2,128,3072]{3,2,1,0:T(8,128)(2,1)}, u32[]{:S(2)}, u32[]{:S(2)}) collective-permute-start(bf16[2,2,128,3072]{3,2,1,0:T(8,128)(2,1)} %pad_maximum_fusion), channel_id=1, source_target_pairs={{0,1},{1,2},{2,3},{3,4},{4,5},{5,6},{6,7},{7,8},{8,9},{9,10},{10,1... | collective-permute-start | bytes 9437192 | tf_op jit(solution)/shard_map/ppermute | solution.py:21
  93.4 76.0 %copy-start.7 = (bf16[128,3072]{1,0:T(8,128)(2,1)S(1)}, bf16[128,3072]{1,0:T(8,128)(2,1)}, u32[]{:S(2)}) copy-start(bf16[128,3072]{1,0:T(8,128)(2,1)} %get-tuple-element.194) | copy-start | bytes 2359300
  93.4 76.0 %copy-start.8 = (bf16[128,3072]{1,0:T(8,128)(2,1)S(1)}, bf16[128,3072]{1,0:T(8,128)(2,1)}, u32[]{:S(2)}) copy-start(bf16[128,3072]{1,0:T(8,128)(2,1)} %get-tuple-element.200) | copy-start | bytes 2359300
  169.4 5.3 %copy-start.2 = (bf16[4,128,3072]{2,1,0:T(8,128)(2,1)S(1)}, bf16[4,128,3072]{2,1,0:T(8,128)(2,1)}, u32[]{:S(2)}) copy-start(bf16[4,128,3072]{2,1,0:T(8,128)(2,1)} %all-gather.2.cloned.1.call-done) | copy-start | bytes 9437188
  176.9 5.4 %copy-start.10 = (f32[2,24]{1,0:T(2,128)S(1)}, f32[2,24]{1,0:T(2,128)}, u32[]{:S(2)}) copy-start(f32[2,24]{1,0:T(2,128)} %param.13) | copy-start | bytes 580
  190.2 3.1 %copy-start = (f32[24,128,640]{2,1,0:T(8,128)}, f32[24,128,640]{2,1,0:T(8,128)S(1)}, u32[]{:S(2)}) copy-start(f32[24,128,640]{2,1,0:T(8,128)S(1)} %get-tuple-element.185) | copy-start | bytes 23592964 | tf_op jit(solution)/shard_map/conditional.1
Sparse Core Ops, SparseCore 0:
  9.1 63.8 all-gather.1
